TPU v7x, 256 devices: a whole 4x4x8 slice. The times are simulated.
256 devices in a mesh: seq: 64 (over z, y, core), tp: 4 (over x).
Axes of the slice: x: 4, y: 4, z: 8, core: 2. Of those that a mesh axis runs over, the one named last changes fastest.
Arguments:
- normed: bfloat16 [32768, 2048], P('seq', 'tp'), may hold values from -24 to 24
- cluster: int32 [32768, 1], P('seq'), may hold values from 0 to 127; in each aligned block of 512 rows (0 to 511, 512 to 1023, ...) at most 8 rows name the same one
- w_query: bfloat16 [2048, 2048], P(None, 'tp'), may hold values from -1 to 1
- w_key: bfloat16 [2048, 2048], P(None, 'tp'), may hold values from -1 to 1
- w_value: bfloat16 [2048, 2048], P(None, 'tp'), may hold values from -0.125 to 0.125
- w_out: bfloat16 [2048, 2048], P('tp'), may hold values from -0.125 to 0.125
- grad_out: bfloat16 [32768, 2048], P('seq', 'tp'), may hold values from -6 to 6
Outputs:
- attended: bfloat16 [32768, 2048], P('seq', 'tp')
- grad_normed: float32 [32768, 2048], P('seq', 'tp')
Inputs may be any that keep to these rules, and one draw needn't show every extreme that they name: Among the tokens of one index of seq no cluster id appears more than 8 times, and some id appears exactly 8 times; every id appears somewhere.
All inputs are finite; a program needn't handle non-finite values.
Results may differ from a plain program's by a relative error of at most 0.011.
The roundings to bfloat16 on the way count: a program that leaves them out, or rounds other values in their place, can miss the bound.
Values may be sent and summed in bfloat16 or wider, within the bound.
A program may use at most 128 MiB of HBM per device.

v0:
```python
import jax
import jax.numpy as jnp
from jax import lax
from jax.sharding import PartitionSpec as P

HEAD_DIM = 128
CLUSTERS = 128
CAP = 256
MOST = 8


def entering(x, axis, combine, identity):
    count, position = (lax.axis_size(axis), lax.axis_index(axis))
    everything = lax.all_gather(x, axis)
    start = jnp.broadcast_to(jnp.asarray(identity, x.dtype), x.shape)

    def lap(k, before):
        reached = k < position
        new = combine(before, everything[k])
        return jnp.where(reached, new, before)

    return lax.fori_loop(0, count, lap, start)


def cluster_probs(query, key_rows, usable):
    score_scale = query.shape[-1] ** (-0.5)
    scores = (
        jnp.einsum("qhd,khd->hqk", query, key_rows, preferred_element_type=jnp.float32)
        * score_scale
    )
    scores = jnp.where(usable[None, None, :], scores, -1e30)
    row_top = jnp.max(scores, axis=-1, keepdims=True)
    raised = jnp.exp(scores - row_top)
    return raised / jnp.sum(raised, axis=-1, keepdims=True)


def unpack(packed):
    width = packed.shape[1] // 3
    rows = packed.shape[0]
    query = packed[:, :width].reshape(rows, -1, HEAD_DIM)
    key_rows = packed[:, width : 2 * width].reshape(rows, -1, HEAD_DIM)
    value_rows = packed[:, 2 * width :].reshape(rows, -1, HEAD_DIM)
    return (query, key_rows, value_rows)


def forward_one(packed, usable):
    query, key_rows, value_rows = unpack(packed)
    probs = cluster_probs(query, key_rows, usable)
    mixed = jnp.einsum(
        "hqk,khd->qhd", probs.astype(jnp.bfloat16), value_rows, preferred_element_type=jnp.float32
    )
    return mixed.reshape(packed.shape[0], -1).astype(jnp.bfloat16)


def attention_core(packed, usable, grad_rows):
    query, key_rows, value_rows = unpack(packed)
    rows = packed.shape[0]
    score_scale = query.shape[-1] ** (-0.5)
    grad_heads = grad_rows.reshape(rows, -1, HEAD_DIM)
    probs = cluster_probs(query, key_rows, usable)
    rounded = probs.astype(jnp.bfloat16)
    mixed = jnp.einsum("hqk,khd->qhd", rounded, value_rows, preferred_element_type=jnp.float32)
    grad_value = jnp.einsum("hqk,qhd->khd", rounded, grad_heads, preferred_element_type=jnp.float32)
    grad_probs = jnp.einsum(
        "qhd,khd->hqk", grad_heads, value_rows, preferred_element_type=jnp.float32
    )
    inner = jnp.sum(grad_probs * probs, axis=-1, keepdims=True)
    grad_scores = (probs * (grad_probs - inner) * score_scale).astype(jnp.bfloat16)
    grad_query = jnp.einsum(
        "hqk,khd->qhd", grad_scores, key_rows, preferred_element_type=jnp.float32
    )
    grad_key = jnp.einsum("hqk,qhd->khd", grad_scores, query, preferred_element_type=jnp.float32)
    grads = jnp.concatenate(
        [
            grad_query.reshape(rows, -1).astype(jnp.bfloat16),
            grad_key.reshape(rows, -1).astype(jnp.bfloat16),
            grad_value.reshape(rows, -1).astype(jnp.bfloat16),
        ],
        axis=1,
    )
    return (mixed.reshape(rows, -1).astype(jnp.bfloat16), grads)


def body(normed, cluster, w_query, w_key, w_value, w_out, grad_out):
    seq_count = lax.axis_size("seq")
    local_cols = w_query.shape[1]
    cluster_here = CLUSTERS // seq_count
    cluster_ids = cluster[:, 0]
    columns = jnp.arange(CLUSTERS, dtype=jnp.int32)
    one_hot = (cluster_ids[:, None] == columns[None, :]).astype(jnp.int32)
    running = jnp.cumsum(one_hot, axis=0)
    local_rank = jnp.sum((running - one_hot) * one_hot, axis=1)
    counts = running[-1]
    offsets = entering(
        counts, "seq", lambda earlier, later: earlier + later, jnp.zeros_like(counts)
    )
    global_rank = local_rank + jnp.sum(one_hot * offsets[None, :], axis=1)
    kept_rows = (global_rank < CAP).astype(jnp.bfloat16)
    slot_index = cluster_ids * MOST + local_rank
    piece = lax.all_gather(normed, "tp", axis=1, tiled=True)
    query_sum = jnp.dot(piece, w_query, preferred_element_type=jnp.float32)
    key_sum = jnp.dot(piece, w_key, preferred_element_type=jnp.float32)
    value_sum = jnp.dot(piece, w_value, preferred_element_type=jnp.float32)
    packed_rows = jnp.concatenate(
        [
            query_sum.astype(jnp.bfloat16),
            key_sum.astype(jnp.bfloat16),
            value_sum.astype(jnp.bfloat16),
        ],
        axis=1,
    )
    head_grads = (
        lax.dot_general(
            lax.all_gather(grad_out, "tp", axis=1, tiled=True),
            w_out,
            (((1,), (1,)), ((), ())),
            preferred_element_type=jnp.float32,
        ).astype(jnp.bfloat16)
        * kept_rows[:, None]
    )

    def to_owners(rows):
        buffer = jnp.zeros((CLUSTERS * MOST, rows.shape[1]), rows.dtype).at[slot_index].set(rows)
        return buffer.reshape(seq_count, cluster_here, MOST, rows.shape[1])

    flags = (
        jnp.zeros((CLUSTERS * MOST,), jnp.bfloat16)
        .at[slot_index]
        .set(kept_rows)
        .reshape(seq_count, cluster_here, MOST)
    )

    def from_owners(slots):
        return slots.reshape(cluster_here, seq_count, MOST, slots.shape[-1])

    def to_tokens(returned):
        return (
            returned.reshape(CLUSTERS * MOST, returned.shape[-1])[slot_index] * kept_rows[:, None]
        )

    arrived, arrived_flags = (
        lax.all_to_all(to_owners(packed_rows), "seq", split_axis=0, concat_axis=2, tiled=True),
        lax.all_to_all(flags, "seq", split_axis=0, concat_axis=2, tiled=True),
    )
    usable = arrived_flags[0] > 0
    mixed_slots = lax.map(lambda pair: forward_one(pair[0], pair[1]), (arrived[0], usable))
    heads_tok = to_tokens(
        lax.all_to_all(from_owners(mixed_slots), "seq", split_axis=1, concat_axis=0, tiled=True)
    )
    grad_arrived = lax.all_to_all(
        to_owners(head_grads), "seq", split_axis=0, concat_axis=2, tiled=True
    )
    grad_slots = lax.map(
        lambda triple: attention_core(triple[0], triple[1], triple[2])[1],
        (arrived[0], usable, grad_arrived[0]),
    )
    grads_tok = to_tokens(
        lax.all_to_all(from_owners(grad_slots), "seq", split_axis=1, concat_axis=0, tiled=True)
    )
    partial_out = jnp.dot(heads_tok, w_out, preferred_element_type=jnp.float32)
    attended = lax.psum_scatter(partial_out, "tp", scatter_dimension=1, tiled=True).astype(
        jnp.bfloat16
    )
    contract = (((1,), (1,)), ((), ()))
    partial_grad = lax.dot_general(
        grads_tok[:, :local_cols], w_query, contract, preferred_element_type=jnp.float32
    )
    partial_grad = partial_grad + lax.dot_general(
        grads_tok[:, local_cols : 2 * local_cols],
        w_key,
        contract,
        preferred_element_type=jnp.float32,
    )
    partial_grad = partial_grad + lax.dot_general(
        grads_tok[:, 2 * local_cols :], w_value, contract, preferred_element_type=jnp.float32
    )
    grad_normed = lax.psum_scatter(partial_grad, "tp", scatter_dimension=1, tiled=True)
    return (attended, grad_normed)


def solution(mesh):
    in_specs = (
        P("seq", "tp"),
        P("seq", None),
        P(None, "tp"),
        P(None, "tp"),
        P(None, "tp"),
        P("tp", None),
        P("seq", "tp"),
    )
    out_specs = (P("seq", "tp"), P("seq", "tp"))
    return jax.shard_map(body, mesh=mesh, in_specs=in_specs, out_specs=out_specs, check_vma=False)
```

profile of v0, /device:TPU:1, one launch (start us, length us, event | category | flops | bytes accessed | tf_op | source)
XLA Modules:
  0.0 460.2 jit_solution(15803309775498486307)
XLA Ops:
  7.9 0.8 copy.71
  9.0 44.2 %all-gather = s32[64,1,128]{2,1,0:T(1,128)S(1)} all-gather(s32[1,1,128]{2,1,0:T(1,128)S(1)} %slice_bitcast_fusion.1), channel_id=1, replica_groups=mesh['seq'=64,'tp'=4] {'seq'}, dimensions={0}, use_global_device_ids=true | all-gather | bytes 33280 | tf_op jit(solution)/shard_map/all_gather | solution.py:14
  53.3 2.6 while.36
  55.9 1.0 select_reduce_fusion
  57.5 3.8 scatter_custom_fusion.1
  61.3 0.7 reshape.110
  62.0 6.8 %all-to-all-start.1 = ((bf16[64,2,8]{2,1,0:T(2,128)(2,1)}), bf16[64,2,8]{2,1,0:T(2,128)(2,1)S(1)}, u32[]{:S(2)}, u32[]{:S(2)}) async-start(bf16[64,2,8]{2,1,0:T(2,128)(2,1)} %reshape.110), calls=%async_computation.1 | async-start | bytes 65536 | tf_op jit(solution)/shard_map/all_to_all | solution.py:143
  68.9 3.7 convolution_convert_fusion.1
  72.6 1.3 convolution_convert_fusion.2
  74.2 1.3 convolution_convert_fusion.3
  75.5 1.2 pad_maximum_fusion
  76.8 2.6 copy.73
  79.4 6.0 %scatter_custom_fusion = bf16[1024,1536]{1,0:T(8,128)(2,1)} fusion(s32[512]{0:T(512)S(1)} %bitcast.181, bf16[512,1536]{1,0:T(8,128)(2,1)} %copy.73, bf16[]{:T(256)} %constant.82.clone.1), kind=kCustom, calls=%fused_computation.59 | custom fusion | bytes 3146240 | tf_op jit(solution)/shard_map/scatter | solution.py:123
  85.4 10.5 %all-to-all-start = ((bf16[64,2,8,1536]{3,2,1,0:T(8,128)(2,1)}), bf16[64,2,8,1536]{3,2,1,0:T(8,128)(2,1)}, u32[]{:S(2)}, u32[]{:S(2)}) async-start(bf16[64,2,8,1536]{3,2,1,0:T(8,128)(2,1)} %bitcast.169), calls=%async_computation | async-start | bytes 6291456 | tf_op jit(solution)/shard_map/all_to_all | solution.py:142
  96.8 36.0 %all-gather.6.cloned.1.call-done = bf16[512,2048]{1,0:T(8,128)(2,1)} async-done(((bf16[512,512]{1,0:T(8,128)(2,1)}), bf16[512,2048]{1,0:T(8,128)(2,1)}) %all-gather.6.cloned.1.call-update) | async-done | bytes 2097168 | tf_op jit(solution)/shard_map/all_gather | solution.py:114
  132.8 2.9 fusion.49
  135.7 3.5 scatter_custom_fusion.2
  139.2 29.2 %all-to-all-done = bf16[64,2,8,1536]{3,2,1,0:T(8,128)(2,1)} async-done(((bf16[64,2,8,1536]{3,2,1,0:T(8,128)(2,1)}), bf16[64,2,8,1536]{3,2,1,0:T(8,128)(2,1)}, u32[]{:S(2)}, u32[]{:S(2)}) %all-to-all-start) | async-done | bytes 3145760 | tf_op jit(solution)/shard_map/all_to_all | solution.py:142
  168.3 6.8 %all-to-all-start.3 = ((bf16[64,2,8,512]{3,2,1,0:T(8,128)(2,1)}), bf16[64,2,8,512]{3,2,1,0:T(8,128)(2,1)}, u32[]{:S(2)}, u32[]{:S(2)}) async-start(bf16[64,2,8,512]{3,2,1,0:T(8,128)(2,1)} %bitcast.38), calls=%async_computation.4 | async-start | bytes 2097152 | tf_op jit(solution)/shard_map/all_to_all | solution.py:150
  175.1 3.8 copy_bitcast_fusion
  179.0 4.7 %copy.76 = bf16[2,512,1536]{1,2,0:T(8,128)(2,1)} copy(bf16[2,512,1536]{2,1,0:T(8,128)(2,1)} %copy_bitcast_fusion) | data formatting | bytes 6291456 | tf_op jit(solution)/shard_map/while | solution.py:146
  183.7 21.6 %while.34 = (s32[]{:T(128)}, bf16[2,512,512]{2,1,0:T(8,128)(2,1)}, bf16[2,512,1536]{1,2,0:T(8,128)(2,1)}, pred[2,512]{1,0:T(4,128)(4,1)S(1)}, s32[]{:T(128)}) while((s32[]{:T(128)}, bf16[2,512,512]{2,1,0:T(8,128)(2,1)}, bf16[2,512,1536]{1,2,0:T(8,128)(2,1)}, pred[2,512]{1,0:T(4,128)(4,1)S(1)}, s32[]{:T(128)}) %tuple.85), condition=%wide.region_11.12_spmd, body=%wide.region_8.11_spmd.sunk | while | flops 543425024 | bytes 18892868 | solution.py:146
  183.7 1.5 dynamic-slice_bitcast_fusion.4
  185.2 0.9 fusion.124
  186.1 4.7 %fusion.125 = (f32[4,512]{1,0:T(4,128)S(1)}, f32[4,512,512]{1,2,0:T(8,128)}) fusion(pred[512]{0:T(512)(128)(4,1)S(1)} %dynamic-slice_reduce_fusion.4, bf16[512,4,128]{0,2,1:T(8,128)(2,1)} %bitcast.166, bf16[512,4,128]{0,2,1:T(8,128)(2,1)S(1)} %bitcast.165), kind=kOutput, calls=%fused_computation.96.clone.1 | convolution fusion | flops 272630272 | bytes 5251584 | tf_op jit(solution)/shard_map/while/body/eval_jaxpr/sub | solution.py:33
  190.8 2.6 fusion.126
  193.6 0.8 constant_dynamic-update-slice_fusion.4
  194.5 1.5 dynamic-slice_bitcast_fusion.4
  196.0 0.9 fusion.124
  196.9 4.7 %fusion.125 = (f32[4,512]{1,0:T(4,128)S(1)}, f32[4,512,512]{1,2,0:T(8,128)}) fusion(pred[512]{0:T(512)(128)(4,1)S(1)} %dynamic-slice_reduce_fusion.4, bf16[512,4,128]{0,2,1:T(8,128)(2,1)} %bitcast.166, bf16[512,4,128]{0,2,1:T(8,128)(2,1)S(1)} %bitcast.165), kind=kOutput, calls=%fused_computation.96.clone.1 | convolution fusion | flops 272630272 | bytes 5251584 | tf_op jit(solution)/shard_map/while/body/eval_jaxpr/sub | solution.py:33
  201.6 2.6 fusion.126
  204.4 0.8 constant_dynamic-update-slice_fusion.4
  205.2 2.4 copy.78
  207.7 10.3 %all-to-all-start.2 = ((bf16[2,64,8,512]{3,2,0,1:T(8,128)(2,1)}), bf16[2,64,8,512]{3,2,0,1:T(8,128)(2,1)S(1)}, u32[]{:S(2)}, u32[]{:S(2)}) async-start(bf16[2,64,8,512]{3,2,0,1:T(8,128)(2,1)} %copy.78), calls=%async_computation.2 | async-start | bytes 2097152 | tf_op jit(solution)/shard_map/all_to_all | solution.py:148
  218.1 2.3 copy_bitcast_fusion.1
  220.4 25.6 %all-to-all-done.2 = bf16[2,64,8,512]{3,2,0,1:T(8,128)(2,1)S(1)} async-done(((bf16[2,64,8,512]{3,2,0,1:T(8,128)(2,1)}), bf16[2,64,8,512]{3,2,0,1:T(8,128)(2,1)S(1)}, u32[]{:S(2)}, u32[]{:S(2)}) %all-to-all-start.2) | async-done | bytes 1048608 | tf_op jit(solution)/shard_map/all_to_all | solution.py:148
  246.0 2.6 gather_fusion
  248.6 4.3 fusion.57
  253.1 60.3 %while.35 = (s32[]{:T(128)}, bf16[2,512,1536]{2,1,0:T(8,128)(2,1)}, bf16[2,512,1536]{1,2,0:T(8,128)(2,1)}, pred[2,512]{1,0:T(4,128)(4,1)S(1)}, bf16[2,512,512]{2,1,0:T(8,128)(2,1)}, /*index=5*/s32[]{:T(128)}) while((s32[]{:T(128)}, bf16[2,512,1536]{2,1,0:T(8,128)(2,1)}, bf16[2,512,1536]{1,2,0:T(8,128)(2,1)}, pred[2,512]{1,0:T(4,128)(4,1)S(1)}, ...), condition=%wide.region_18.19_spmd, body=%wide.region_14.18_spmd.sunk | while | flops 1368659456 | bytes 52463696 | solution.py:153
  253.1 1.5 dynamic-slice_bitcast_fusion.5
  254.8 3.7 fusion.138
  258.5 1.1 constant_dynamic-slice_fusion.2
  259.7 2.9 fusion.140
  262.7 7.8 %fusion.142 = bf16[4,128,512]{2,1,0:T(8,128)(2,1)S(1)} fusion(bf16[512,4,128]{0,2,1:T(8,128)(2,1)S(1)} %bitcast.162, f32[4,512,512]{1,2,0:T(8,128)} %fusion.140, f32[4,512,512]{1,2,0:T(8,128)} %get-tuple-element.302, f32[4,512]{1,0:T(4,128)S(1)} %get-tuple-element.303), kind=kOutput, calls=%fused_computation.44.clone.1 | convolution fusion | flops 276040192 | bytes 9445376 | tf_op jit(solution)/shard_map/while/body/eval_jaxpr/hqk,khd->qhd/dot_general | solution.py:69
  270.5 7.7 %fusion.141 = bf16[4,128,512]{2,1,0:T(8,128)(2,1)S(1)} fusion(bf16[512,4,128]{0,2,1:T(8,128)(2,1)S(1)} %bitcast.160, f32[4,512,512]{1,2,0:T(8,128)} %fusion.140, f32[4,512,512]{1,2,0:T(8,128)} %get-tuple-element.302, f32[4,512]{1,0:T(4,128)S(1)} %get-tuple-element.303), kind=kOutput, calls=%fused_computation.45.clone.1 | convolution fusion | flops 276040192 | bytes 9445376 | tf_op jit(solution)/shard_map/while/body/eval_jaxpr/hqk,qhd->khd/dot_general | solution.py:72
  278.2 3.1 fusion.139
  282.1 1.3 constant_dynamic-update-slice_fusion.5
  283.4 1.5 dynamic-slice_bitcast_fusion.5
  285.0 3.7 fusion.138
  288.7 1.1 constant_dynamic-slice_fusion.2
  290.0 2.7 fusion.140
  292.7 7.9 %fusion.142 = bf16[4,128,512]{2,1,0:T(8,128)(2,1)S(1)} fusion(bf16[512,4,128]{0,2,1:T(8,128)(2,1)S(1)} %bitcast.162, f32[4,512,512]{1,2,0:T(8,128)} %fusion.140, f32[4,512,512]{1,2,0:T(8,128)} %get-tuple-element.302, f32[4,512]{1,0:T(4,128)S(1)} %get-tuple-element.303), kind=kOutput, calls=%fused_computation.44.clone.1 | convolution fusion | flops 276040192 | bytes 9445376 | tf_op jit(solution)/shard_map/while/body/eval_jaxpr/hqk,khd->qhd/dot_general | solution.py:69
  300.6 7.6 %fusion.141 = bf16[4,128,512]{2,1,0:T(8,128)(2,1)S(1)} fusion(bf16[512,4,128]{0,2,1:T(8,128)(2,1)S(1)} %bitcast.160, f32[4,512,512]{1,2,0:T(8,128)} %fusion.140, f32[4,512,512]{1,2,0:T(8,128)} %get-tuple-element.302, f32[4,512]{1,0:T(4,128)S(1)} %get-tuple-element.303), kind=kOutput, calls=%fused_computation.45.clone.1 | convolution fusion | flops 276040192 | bytes 9445376 | tf_op jit(solution)/shard_map/while/body/eval_jaxpr/hqk,qhd->khd/dot_general | solution.py:72
  308.2 3.0 fusion.139
  312.1 1.3 constant_dynamic-update-slice_fusion.5
  313.4 2.3 copy.83
  315.7 79.5 %all_to_all.69 = bf16[2,64,8,1536]{3,2,0,1:T(8,128)(2,1)S(1)} all-to-all(bf16[2,64,8,1536]{3,2,0,1:T(8,128)(2,1)S(1)} %copy.83), channel_id=1, replica_groups=mesh['seq'=64,'tp'=4] {'seq'}, dimensions={1} | all-to-all | bytes 6291456 | tf_op jit(solution)/shard_map/all_to_all | solution.py:158
  395.2 3.0 gather_fusion.1
  398.1 1.7 broadcast_multiply_fusion
  400.2 1.3 fusion.51
  401.8 1.3 fusion.53
  403.4 3.3 add_add_fusion
  406.7 2.1 convert_element_type.87
  408.8 44.7 %reduce-scatter.5.cloned.1.call-done = f32[512,512]{1,0:T(8,128)} async-done(((f32[512,2048]{1,0:T(8,128)}), f32[512,512]{1,0:T(8,128)}) %reduce-scatter.5.cloned.1.call-update) | async-done | bytes 1048592 | tf_op jit(solution)/shard_map/reduce_scatter | solution.py:177
  (123 shorter events, 8.1 us)
Async XLA Ops:
  7.2 125.7 %copy-start = (bf16[512,2048]{1,0:T(8,128)(2,1)S(1)}, bf16[512,2048]{1,0:T(8,128)(2,1)}, u32[]{:S(2)}) copy-start(bf16[512,2048]{1,0:T(8,128)(2,1)} %param.18) | copy-start | bytes 6291460
  7.2 61.7 %all-gather.4.cloned.1.call-start = ((), (), s32[]{:S(2)}) async-start(), calls=%async_computation.7 | async-start | bytes 2621440 | tf_op jit(solution)/shard_map/all_gather | solution.py:100
  62.0 23.3 %all-to-all-start.1 = ((bf16[64,2,8]{2,1,0:T(2,128)(2,1)}), bf16[64,2,8]{2,1,0:T(2,128)(2,1)S(1)}, u32[]{:S(2)}, u32[]{:S(2)}) async-start(bf16[64,2,8]{2,1,0:T(2,128)(2,1)} %reshape.110), calls=%async_computation.1 | async-start | bytes 65536 | tf_op jit(solution)/shard_map/all_to_all | solution.py:143
  68.9 3.7 copy-start.2
  68.9 3.7 copy-start.7
  72.6 1.6 copy-start.4
  85.4 83.0 %all-to-all-start = ((bf16[64,2,8,1536]{3,2,1,0:T(8,128)(2,1)}), bf16[64,2,8,1536]{3,2,1,0:T(8,128)(2,1)}, u32[]{:S(2)}, u32[]{:S(2)}) async-start(bf16[64,2,8,1536]{3,2,1,0:T(8,128)(2,1)} %bitcast.169), calls=%async_computation | async-start | bytes 6291456 | tf_op jit(solution)/shard_map/all_to_all | solution.py:142
  95.8 37.0 %all-gather.6.cloned.1.call-start = ((), (), s32[]{:S(2)}) async-start(), calls=%async_computation.9 | async-start | bytes 2621440 | tf_op jit(solution)/shard_map/all_gather | solution.py:114
  168.3 39.4 %all-to-all-start.3 = ((bf16[64,2,8,512]{3,2,1,0:T(8,128)(2,1)}), bf16[64,2,8,512]{3,2,1,0:T(8,128)(2,1)}, u32[]{:S(2)}, u32[]{:S(2)}) async-start(bf16[64,2,8,512]{3,2,1,0:T(8,128)(2,1)} %bitcast.38), calls=%async_computation.4 | async-start | bytes 2097152 | tf_op jit(solution)/shard_map/all_to_all | solution.py:150
  207.7 38.3 %all-to-all-start.2 = ((bf16[2,64,8,512]{3,2,0,1:T(8,128)(2,1)}), bf16[2,64,8,512]{3,2,0,1:T(8,128)(2,1)S(1)}, u32[]{:S(2)}, u32[]{:S(2)}) async-start(bf16[2,64,8,512]{3,2,0,1:T(8,128)(2,1)} %copy.78), calls=%async_computation.2 | async-start | bytes 2097152 | tf_op jit(solution)/shard_map/all_to_all | solution.py:148
  218.0 188.7 %reduce-scatter.3.cloned.1.call-start = ((), (), s32[]{:S(2)}) async-start(), calls=%async_computation.8 | async-start | bytes 5242880 | tf_op jit(solution)/shard_map/reduce_scatter | solution.py:161
  252.9 200.6 %reduce-scatter.5.cloned.1.call-start = ((), (), s32[]{:S(2)}) async-start(), calls=%async_computation.10 | async-start | bytes 5242880 | tf_op jit(solution)/shard_map/reduce_scatter | solution.py:177
  398.1 2.1 copy-start.3
  400.2 1.6 copy-start.5
  401.8 1.6 copy-start.6
  403.4 50.1 %copy-start.1 = (bf16[512,2048]{1,0:T(8,128)(2,1)S(1)}, bf16[512,2048]{1,0:T(8,128)(2,1)}, u32[]{:S(2)}) copy-start(bf16[512,2048]{1,0:T(8,128)(2,1)} %param.18) | copy-start | bytes 6291460
Sparse Core Ops, SparseCore 0:
  9.8 37.1 all-gather.3
  98.5 34.2 all-gather.5
  253.0 46.4 reduce-scatter.2
  406.8 46.6 reduce-scatter.4
where the time goes:
time: 466 us; the launch traced here: 460 us
  waiting for transfers between devices  136 us (29%)
  blocking collectives  124 us (27%)
  matrix products  83.9 us (18%)
  local copies, waits for them, and re-layouts  56.7 us (12%)
  starting transfers between devices  35.3 us (8%)
  between operations  14.3 us (3%)
  other arithmetic  8.37 us (2%)
    all_to_all x1, blocking collectives, body(): lax.all_to_all(from_owners(grad_slots), 'seq', split_axis=1, concat_axis=...  79.5 us
    reduce_scatter x1, waiting for transfers between devices, body(): lax.psum_scatter(partial_grad, 'tp', scatter_dimension=1, tiled=True)  44.7 us
    all_gather x1, blocking collectives, entering(): everything = lax.all_gather(x, axis)  44.2 us
    all_gather x1, waiting for transfers between devices, body(): lax.all_gather(grad_out, 'tp', axis=1, tiled=True)  36 us
    all_to_all x1, waiting for transfers between devices, body(): lax.all_to_all(to_owners(packed_rows), 'seq', split_axis=0, concat_axis=2...  29.2 us
    all_to_all x1, waiting for transfers between devices, body(): lax.all_to_all(from_owners(mixed_slots), 'seq', split_axis=1, concat_axis...  25.6 us
    sub x4, matrix products, cluster_probs(): raised = jnp.exp(scores - row_top)  16.6 us
    dot_general x2, matrix products, attention_core(): jnp.einsum('hqk,khd->qhd', grad_scores, key_rows, preferred_element_type=...  15.7 us
  transfers between devices with their start and end apart: 8, of which 4 were waited for; matrix products, arithmetic and copies ran while one was open for 31% of the time, Pallas kernels for 0%

commit v1 on v0

--- a/solution.py
+++ b/solution.py
@@ -111,7 +111,9 @@
     )
     head_grads = (
         lax.dot_general(
-            lax.all_gather(grad_out, "tp", axis=1, tiled=True),
+            jnp.concatenate(
+                lax.all_to_all(jnp.stack([grad_out] * lax.axis_size("tp")), "tp", 0, 0), axis=1
+            ),
             w_out,
             (((1,), (1,)), ((), ())),
             preferred_element_type=jnp.float32,

time: 466 us -> 486 us (1.043)
  waiting for transfers between devices: 136 us -> 153 us
    all_to_all x1, waiting for transfers between devices: 29.2 us -> 66 us  [body(): lax.all_to_all(to_owners(packed_rows), 'seq', split_axis=0, concat_axis=2...]
    all_gather x1 -> x0, waiting for transfers between devices: 36 us -> none  [body(): lax.all_gather(grad_out, 'tp', axis=1, tiled=True)]
    all_to_all x0 -> x1, waiting for transfers between devices: none -> 9.25 us  [body(): lax.all_to_all(jnp.stack([grad_out] * lax.axis_size('tp')), 'tp', 0, 0)]
    all_to_all x1, waiting for transfers between devices: 0.01 us -> 8.04 us  [body(): lax.all_to_all(flags, 'seq', split_axis=0, concat_axis=2, tiled=True)]
  transfers between devices with their start and end apart: 8 -> 8, of which waited for: 4 -> 5; matrix products, arithmetic and copies ran while one was open for 31% -> 30% of each run, Pallas kernels for 0% -> 0%
where the time goes in v1:
time: 486 us; the launch traced here: 479 us
  waiting for transfers between devices  153 us (31%)
  blocking collectives  124 us (26%)
  matrix products  83.7 us (17%)
  local copies, waits for them, and re-layouts  59.5 us (12%)
  starting transfers between devices  35.7 us (7%)
  between operations  14.3 us (3%)
  other arithmetic  8.37 us (2%)
    all_to_all x1, blocking collectives, body(): lax.all_to_all(from_owners(grad_slots), 'seq', split_axis=1, concat_axis=...  79.5 us
    all_to_all x1, waiting for transfers between devices, body(): lax.all_to_all(to_owners(packed_rows), 'seq', split_axis=0, concat_axis=2...  66 us
    all_gather x1, blocking collectives, entering(): everything = lax.all_gather(x, axis)  44.2 us
    reduce_scatter x1, waiting for transfers between devices, body(): lax.psum_scatter(partial_grad, 'tp', scatter_dimension=1, tiled=True)  43 us
    all_to_all x1, waiting for transfers between devices, body(): lax.all_to_all(from_owners(mixed_slots), 'seq', split_axis=1, concat_axis...  25.6 us
    sub x4, matrix products, cluster_probs(): raised = jnp.exp(scores - row_top)  16.6 us
    dot_general x2, matrix products, attention_core(): jnp.einsum('hqk,khd->qhd', grad_scores, key_rows, preferred_element_type=...  15.7 us
    dot_general x2, matrix products, attention_core(): jnp.einsum('hqk,qhd->khd', grad_scores, query, preferred_element_type=jnp...  15.3 us
  transfers between devices with their start and end apart: 8, of which 5 were waited for; matrix products, arithmetic and copies ran while one was open for 30% of the time, Pallas kernels for 0%

profile of v1, /device:TPU:1, one launch (start us, length us, event | category | flops | bytes accessed | tf_op | source)
XLA Modules:
  0.0 479.4 jit_solution(12188896048590406434)
XLA Ops:
  9.0 44.2 %all-gather = s32[64,1,128]{2,1,0:T(1,128)S(1)} all-gather(s32[1,1,128]{2,1,0:T(1,128)S(1)} %slice_bitcast_fusion.1), channel_id=1, replica_groups=mesh['seq'=64,'tp'=4] {'seq'}, dimensions={0}, use_global_device_ids=true | all-gather | bytes 33280 | tf_op jit(solution)/shard_map/all_gather | solution.py:14
  53.3 2.6 while.36
  55.9 1.0 select_reduce_fusion
  57.5 3.8 scatter_custom_fusion.1
  62.0 6.4 %all-to-all-start.1 = ((bf16[64,2,8]{2,1,0:T(2,128)(2,1)}), bf16[64,2,8]{2,1,0:T(2,128)(2,1)S(1)}, u32[]{:S(2)}, u32[]{:S(2)}) async-start(bf16[64,2,8]{2,1,0:T(2,128)(2,1)} %reshape.118), calls=%async_computation.1 | async-start | bytes 65536 | tf_op jit(solution)/shard_map/all_to_all | solution.py:145
  68.5 1.3 copy.81
  69.7 8.0 %all-to-all-done.1 = bf16[64,2,8]{2,1,0:T(2,128)(2,1)S(1)} async-done(((bf16[64,2,8]{2,1,0:T(2,128)(2,1)}), bf16[64,2,8]{2,1,0:T(2,128)(2,1)S(1)}, u32[]{:S(2)}, u32[]{:S(2)}) %all-to-all-start.1) | async-done | bytes 2080 | tf_op jit(solution)/shard_map/all_to_all | solution.py:145
  77.8 1.5 stack.2
  79.3 4.8 all-to-all-start.3
  84.1 3.7 convolution_convert_fusion.1
  87.8 1.3 convolution_convert_fusion.2
  89.4 1.3 convolution_convert_fusion.3
  90.7 1.3 pad_maximum_fusion
  91.9 2.6 copy.75
  94.6 6.0 %scatter_custom_fusion = bf16[1024,1536]{1,0:T(8,128)(2,1)} fusion(s32[512]{0:T(512)S(1)} %bitcast.184, bf16[512,1536]{1,0:T(8,128)(2,1)} %copy.75, bf16[]{:T(256)} %constant.82.clone.1), kind=kCustom, calls=%fused_computation.59 | custom fusion | bytes 3146240 | tf_op jit(solution)/shard_map/scatter | solution.py:125
  100.6 9.3 %all-to-all-done.3 = bf16[4,512,512]{1,2,0:T(8,128)(2,1)} async-done(((bf16[4,512,512]{1,2,0:T(8,128)(2,1)}), bf16[4,512,512]{1,2,0:T(8,128)(2,1)}, u32[]{:S(2)}, u32[]{:S(2)}) %all-to-all-start.3) | async-done | bytes 2097184 | tf_op jit(solution)/shard_map/all_to_all | solution.py:115
  109.8 7.2 %all-to-all-start = ((bf16[64,2,8,1536]{3,2,1,0:T(8,128)(2,1)}), bf16[64,2,8,1536]{3,2,1,0:T(8,128)(2,1)}, u32[]{:S(2)}, u32[]{:S(2)}) async-start(bf16[64,2,8,1536]{3,2,1,0:T(8,128)(2,1)} %bitcast.172), calls=%async_computation | async-start | bytes 6291456 | tf_op jit(solution)/shard_map/all_to_all | solution.py:144
  117.2 2.9 fusion.49
  120.1 3.5 scatter_custom_fusion.2
  123.6 66.0 %all-to-all-done = bf16[64,2,8,1536]{3,2,1,0:T(8,128)(2,1)} async-done(((bf16[64,2,8,1536]{3,2,1,0:T(8,128)(2,1)}), bf16[64,2,8,1536]{3,2,1,0:T(8,128)(2,1)}, u32[]{:S(2)}, u32[]{:S(2)}) %all-to-all-start) | async-done | bytes 3145760 | tf_op jit(solution)/shard_map/all_to_all | solution.py:144
  189.6 6.7 %all-to-all-start.4 = ((bf16[64,2,8,512]{3,2,1,0:T(8,128)(2,1)}), bf16[64,2,8,512]{3,2,1,0:T(8,128)(2,1)}, u32[]{:S(2)}, u32[]{:S(2)}) async-start(bf16[64,2,8,512]{3,2,1,0:T(8,128)(2,1)} %bitcast.40), calls=%async_computation.5 | async-start | bytes 2097152 | tf_op jit(solution)/shard_map/all_to_all | solution.py:152
  196.3 3.8 copy_bitcast_fusion
  200.1 4.7 copy.78
  204.8 21.6 %while.34 = (s32[]{:T(128)}, bf16[2,512,512]{2,1,0:T(8,128)(2,1)}, bf16[2,512,1536]{1,2,0:T(8,128)(2,1)}, pred[2,512]{1,0:T(4,128)(4,1)S(1)}, s32[]{:T(128)}) while((s32[]{:T(128)}, bf16[2,512,512]{2,1,0:T(8,128)(2,1)}, bf16[2,512,1536]{1,2,0:T(8,128)(2,1)}, pred[2,512]{1,0:T(4,128)(4,1)S(1)}, s32[]{:T(128)}) %tuple.85), condition=%wide.region_11.12_spmd, body=%wide.region_8.11_spmd.sunk | while | flops 543425024 | bytes 18892868 | solution.py:148
  204.8 1.5 dynamic-slice_bitcast_fusion.4
  206.3 0.9 fusion.124
  207.2 4.7 fusion.125
  211.9 2.6 fusion.126
  215.6 1.5 dynamic-slice_bitcast_fusion.4
  217.1 0.9 fusion.124
  218.0 4.7 fusion.125
  222.7 2.6 fusion.126
  226.4 2.4 copy.80
  228.8 10.3 %all-to-all-start.2 = ((bf16[2,64,8,512]{3,2,0,1:T(8,128)(2,1)}), bf16[2,64,8,512]{3,2,0,1:T(8,128)(2,1)S(1)}, u32[]{:S(2)}, u32[]{:S(2)}) async-start(bf16[2,64,8,512]{3,2,0,1:T(8,128)(2,1)} %copy.80), calls=%async_computation.2 | async-start | bytes 2097152 | tf_op jit(solution)/shard_map/all_to_all | solution.py:150
  239.2 2.3 copy_bitcast_fusion.1
  241.5 25.6 %all-to-all-done.2 = bf16[2,64,8,512]{3,2,0,1:T(8,128)(2,1)S(1)} async-done(((bf16[2,64,8,512]{3,2,0,1:T(8,128)(2,1)}), bf16[2,64,8,512]{3,2,0,1:T(8,128)(2,1)S(1)}, u32[]{:S(2)}, u32[]{:S(2)}) %all-to-all-start.2) | async-done | bytes 1048608 | tf_op jit(solution)/shard_map/all_to_all | solution.py:150
  267.1 2.6 gather_fusion
  269.8 4.3 fusion.57
  274.3 60.0 %while.35 = (s32[]{:T(128)}, bf16[2,512,1536]{2,1,0:T(8,128)(2,1)}, bf16[2,512,1536]{1,2,0:T(8,128)(2,1)}, pred[2,512]{1,0:T(4,128)(4,1)S(1)}, bf16[2,512,512]{2,1,0:T(8,128)(2,1)}, /*index=5*/s32[]{:T(128)}) while((s32[]{:T(128)}, bf16[2,512,1536]{2,1,0:T(8,128)(2,1)}, bf16[2,512,1536]{1,2,0:T(8,128)(2,1)}, pred[2,512]{1,0:T(4,128)(4,1)S(1)}, ...), condition=%wide.region_18.19_spmd, body=%wide.region_14.18_spmd.sunk | while | flops 1368659456 | bytes 52463696 | solution.py:155
  274.3 1.5 dynamic-slice_bitcast_fusion.5
  275.9 3.7 fusion.138
  279.6 1.1 constant_dynamic-slice_fusion.2
  280.9 2.7 fusion.140
  283.6 7.8 %fusion.142 = bf16[4,128,512]{2,1,0:T(8,128)(2,1)S(1)} fusion(bf16[512,4,128]{0,2,1:T(8,128)(2,1)S(1)} %bitcast.165, f32[4,512,512]{1,2,0:T(8,128)} %fusion.140, f32[4,512,512]{1,2,0:T(8,128)} %get-tuple-element.302, f32[4,512]{1,0:T(4,128)S(1)} %get-tuple-element.303), kind=kOutput, calls=%fused_computation.44.clone.1 | convolution fusion | flops 276040192 | bytes 9445376 | tf_op jit(solution)/shard_map/while/body/eval_jaxpr/hqk,khd->qhd/dot_general | solution.py:69
  291.5 7.7 %fusion.141 = bf16[4,128,512]{2,1,0:T(8,128)(2,1)S(1)} fusion(bf16[512,4,128]{0,2,1:T(8,128)(2,1)S(1)} %bitcast.163, f32[4,512,512]{1,2,0:T(8,128)} %fusion.140, f32[4,512,512]{1,2,0:T(8,128)} %get-tuple-element.302, f32[4,512]{1,0:T(4,128)S(1)} %get-tuple-element.303), kind=kOutput, calls=%fused_computation.45.clone.1 | convolution fusion | flops 276040192 | bytes 9445376 | tf_op jit(solution)/shard_map/while/body/eval_jaxpr/hqk,qhd->khd/dot_general | solution.py:72
  299.1 3.0 fusion.139
  303.0 1.3 constant_dynamic-update-slice_fusion.5
  304.3 1.6 dynamic-slice_bitcast_fusion.5
  306.0 3.7 fusion.138
  309.6 1.1 constant_dynamic-slice_fusion.2
  310.9 2.7 fusion.140
  313.7 7.9 %fusion.142 = bf16[4,128,512]{2,1,0:T(8,128)(2,1)S(1)} fusion(bf16[512,4,128]{0,2,1:T(8,128)(2,1)S(1)} %bitcast.165, f32[4,512,512]{1,2,0:T(8,128)} %fusion.140, f32[4,512,512]{1,2,0:T(8,128)} %get-tuple-element.302, f32[4,512]{1,0:T(4,128)S(1)} %get-tuple-element.303), kind=kOutput, calls=%fused_computation.44.clone.1 | convolution fusion | flops 276040192 | bytes 9445376 | tf_op jit(solution)/shard_map/while/body/eval_jaxpr/hqk,khd->qhd/dot_general | solution.py:69
  321.6 7.6 %fusion.141 = bf16[4,128,512]{2,1,0:T(8,128)(2,1)S(1)} fusion(bf16[512,4,128]{0,2,1:T(8,128)(2,1)S(1)} %bitcast.163, f32[4,512,512]{1,2,0:T(8,128)} %fusion.140, f32[4,512,512]{1,2,0:T(8,128)} %get-tuple-element.302, f32[4,512]{1,0:T(4,128)S(1)} %get-tuple-element.303), kind=kOutput, calls=%fused_computation.45.clone.1 | convolution fusion | flops 276040192 | bytes 9445376 | tf_op jit(solution)/shard_map/while/body/eval_jaxpr/hqk,qhd->khd/dot_general | solution.py:72
  329.2 3.0 fusion.139
  333.0 1.3 constant_dynamic-update-slice_fusion.5
  334.3 2.3 copy.86
  336.7 79.5 %all_to_all.74 = bf16[2,64,8,1536]{3,2,0,1:T(8,128)(2,1)S(1)} all-to-all(bf16[2,64,8,1536]{3,2,0,1:T(8,128)(2,1)S(1)} %copy.86), channel_id=1, replica_groups=mesh['seq'=64,'tp'=4] {'seq'}, dimensions={1} | all-to-all | bytes 6291456 | tf_op jit(solution)/shard_map/all_to_all | solution.py:160
  416.1 3.0 gather_fusion.1
  419.1 1.7 broadcast_multiply_fusion
  421.1 1.3 fusion.51
  422.7 1.3 fusion.53
  424.3 3.3 add_add_fusion
  427.6 2.1 convert_element_type.87
  429.7 43.0 %reduce-scatter.5.cloned.1.call-done = f32[512,512]{1,0:T(8,128)} async-done(((f32[512,2048]{1,0:T(8,128)}), f32[512,512]{1,0:T(8,128)}) %reduce-scatter.5.cloned.1.call-update) | async-done | bytes 1048592 | tf_op jit(solution)/shard_map/reduce_scatter | solution.py:179
  (124 shorter events, 10.5 us)
Async XLA Ops:
  7.2 110.1 %copy-start = (bf16[512,2048]{1,0:T(8,128)(2,1)S(1)}, bf16[512,2048]{1,0:T(8,128)(2,1)}, u32[]{:S(2)}) copy-start(bf16[512,2048]{1,0:T(8,128)(2,1)} %param.18) | copy-start | bytes 6291460
  7.2 76.9 %all-gather.3.cloned.1.call-start = ((), (), s32[]{:S(2)}) async-start(), calls=%async_computation.8 | async-start | bytes 2621440 | tf_op jit(solution)/shard_map/all_gather | solution.py:100
  62.0 15.7 %all-to-all-start.1 = ((bf16[64,2,8]{2,1,0:T(2,128)(2,1)}), bf16[64,2,8]{2,1,0:T(2,128)(2,1)S(1)}, u32[]{:S(2)}, u32[]{:S(2)}) async-start(bf16[64,2,8]{2,1,0:T(2,128)(2,1)} %reshape.118), calls=%async_computation.1 | async-start | bytes 65536 | tf_op jit(solution)/shard_map/all_to_all | solution.py:145
  79.3 30.5 %all-to-all-start.3 = ((bf16[4,512,512]{1,2,0:T(8,128)(2,1)}), bf16[4,512,512]{1,2,0:T(8,128)(2,1)}, u32[]{:S(2)}, u32[]{:S(2)}) async-start(bf16[4,512,512]{1,2,0:T(8,128)(2,1)} %stack.2), calls=%async_computation.4 | async-start | bytes 4194304 | tf_op jit(solution)/shard_map/all_to_all | solution.py:115
  84.1 3.7 copy-start.2
  84.1 3.7 copy-start.7
  87.8 1.6 copy-start.4
  109.8 79.7 %all-to-all-start = ((bf16[64,2,8,1536]{3,2,1,0:T(8,128)(2,1)}), bf16[64,2,8,1536]{3,2,1,0:T(8,128)(2,1)}, u32[]{:S(2)}, u32[]{:S(2)}) async-start(bf16[64,2,8,1536]{3,2,1,0:T(8,128)(2,1)} %bitcast.172), calls=%async_computation | async-start | bytes 6291456 | tf_op jit(solution)/shard_map/all_to_all | solution.py:144
  189.6 39.3 %all-to-all-start.4 = ((bf16[64,2,8,512]{3,2,1,0:T(8,128)(2,1)}), bf16[64,2,8,512]{3,2,1,0:T(8,128)(2,1)}, u32[]{:S(2)}, u32[]{:S(2)}) async-start(bf16[64,2,8,512]{3,2,1,0:T(8,128)(2,1)} %bitcast.40), calls=%async_computation.5 | async-start | bytes 2097152 | tf_op jit(solution)/shard_map/all_to_all | solution.py:152
  228.8 38.3 %all-to-all-start.2 = ((bf16[2,64,8,512]{3,2,0,1:T(8,128)(2,1)}), bf16[2,64,8,512]{3,2,0,1:T(8,128)(2,1)S(1)}, u32[]{:S(2)}, u32[]{:S(2)}) async-start(bf16[2,64,8,512]{3,2,0,1:T(8,128)(2,1)} %copy.80), calls=%async_computation.2 | async-start | bytes 2097152 | tf_op jit(solution)/shard_map/all_to_all | solution.py:150
  239.1 188.5 %reduce-scatter.3.cloned.1.call-start = ((), (), s32[]{:S(2)}) async-start(), calls=%async_computation.9 | async-start | bytes 5242880 | tf_op jit(solution)/shard_map/reduce_scatter | solution.py:163
  274.0 198.6 %reduce-scatter.5.cloned.1.call-start = ((), (), s32[]{:S(2)}) async-start(), calls=%async_computation.10 | async-start | bytes 5242880 | tf_op jit(solution)/shard_map/reduce_scatter | solution.py:179
  419.1 2.1 copy-start.3
  421.1 1.6 copy-start.5
  422.7 1.6 copy-start.6
  424.3 48.4 %copy-start.1 = (bf16[512,2048]{1,0:T(8,128)(2,1)S(1)}, bf16[512,2048]{1,0:T(8,128)(2,1)}, u32[]{:S(2)}) copy-start(bf16[512,2048]{1,0:T(8,128)(2,1)} %param.18) | copy-start | bytes 6291460
Sparse Core Ops, SparseCore 0:
  9.8 37.1 all-gather.2
  274.2 44.6 reduce-scatter.2
  427.7 44.9 reduce-scatter.4
